TPU v7x, 256 devices: a whole 4x4x8 slice. The times are simulated.
256 devices in a mesh: wide: 64 (over z, x, core), narrow: 4 (over y).
Axes of the slice: x: 4, y: 4, z: 8, core: 2. Of those that a mesh axis runs over, the one named last changes fastest.
Arguments:
- snapshot: float32 [512, 16, 512, 128], P('wide', 'narrow'), may hold values from -81 to 81
Outputs:
- core: float32 [256, 16, 512, 128], P(None, 'narrow', 'wide')
- factor: float32 [512, 256], replicated
All inputs are finite; a program needn't handle non-finite values.
Results may differ from a plain program's by a relative error of at most 0.000071.
Values sent between devices are 32-bit elements; how exact they have to be, the bound alone decides.
A program may use at most 320 MiB of HBM per device.

v0:
```python
import jax
import jax.numpy as jnp
from jax import lax
from jax.sharding import PartitionSpec as P

RANK = 256


def on_device(snapshot):
    regrouped = lax.all_to_all(snapshot, "wide", split_axis=2, concat_axis=0, tiled=True)
    rows_all = regrouped.shape[0]
    unfold = regrouped.reshape(rows_all, -1)
    gram = jnp.dot(
        unfold, unfold.T, precision=lax.Precision.HIGHEST, preferred_element_type=jnp.float32
    )
    gram = lax.psum(gram, "narrow")
    gram = lax.psum(gram, "wide")
    upper = jnp.linalg.cholesky(gram).T
    rows_kept = upper[:RANK, :]
    lengths = jnp.sqrt(jnp.sum(rows_kept * rows_kept, axis=1))
    factor = (rows_kept / lengths[:, None]).T
    core = jnp.dot(
        factor.T, unfold, precision=lax.Precision.HIGHEST, preferred_element_type=jnp.float32
    )
    core = core.reshape(RANK, regrouped.shape[1], regrouped.shape[2], regrouped.shape[3])
    return (core, factor)


def solution(mesh):
    in_specs = (P("wide", "narrow", None, None),)
    out_specs = (P(None, "narrow", "wide", None), P())
    return jax.shard_map(
        on_device, mesh=mesh, in_specs=in_specs, out_specs=out_specs, check_vma=False
    )
```

profile of v0, /device:TPU:1, one launch (start us, length us, event | category | flops | bytes accessed | tf_op | source)
XLA Modules:
  0.0 602.8 jit_solution(17001077467662318990)
XLA Ops:
  7.2 0.0 all-reduce.4.cloned.1.call-start
  7.2 8.2 %copy.21 = f32[8,4,512,128]{3,0,1,2:T(8,128)S(1)} copy(f32[8,4,512,128]{3,2,1,0:T(8,128)} %param.1) | data formatting | bytes 16777216 | tf_op args[0]
  15.4 197.4 %all_to_all.15 = f32[8,4,512,128]{3,0,1,2:T(8,128)S(1)} all-to-all(f32[8,4,512,128]{3,0,1,2:T(8,128)S(1)} %copy.21), channel_id=1, replica_groups=mesh['wide'=64,'narrow'=4] {'wide'}, dimensions={2} | all-to-all | bytes 16777216 | tf_op jit(solution)/shard_map/all_to_all | solution.py:10
  212.9 11.3 %copy.32 = f32[8,4,64,8,128]{4,3,1,0,2:T(8,128)} copy(f32[8,4,64,8,128]{4,0,1,3,2:T(8,128)S(1)} %bitcast.42) | data formatting | bytes 16777216 | tf_op jit(solution)/shard_map/all_to_all | solution.py:10
  224.2 9.4 %reshape.40 = f32[512,4096]{1,0:T(8,128)} reshape(f32[64,8,4,8,128]{4,3,2,1,0:T(8,128)} %bitcast.43) | data formatting | bytes 16777216 | tf_op jit(solution)/shard_map/reshape | solution.py:12
  233.6 17.2 %fusion.15 = f32[512,512]{0,1:T(8,128)} fusion(f32[512,4096]{1,0:T(8,128)} %reshape.40), kind=kOutput, calls=%fused_computation.43 | convolution fusion | flops 12884901888 | bytes 9437184 | tf_op jit(solution)/shard_map/dot_general | solution.py:13
  250.8 0.0 all-reduce.4.cloned.1.call-update
  250.8 0.0 all-reduce.6.cloned.1.call-start
  250.9 47.5 %all-reduce.4.cloned.1.call-done = f32[512,512]{0,1:T(8,128)} async-done(((f32[512,512]{0,1:T(8,128)}), f32[512,512]{0,1:T(8,128)}) %all-reduce.4.cloned.1.call-update) | async-done | bytes 1048592 | tf_op jit(solution)/shard_map/psum | solution.py:16
  298.4 0.0 all-reduce.6.cloned.1.call-update
  298.5 9.4 %copy.25 = f32[4096,512]{1,0:T(8,128)} copy(f32[4096,512]{0,1:T(8,128)} %bitcast.40) | data formatting | bytes 16777216 | tf_op jit(solution)/shard_map/dot_general | solution.py:22
  307.9 180.3 %all-reduce.6.cloned.1.call-done = f32[512,512]{0,1:T(8,128)} async-done(((f32[512,512]{0,1:T(8,128)}), f32[512,512]{0,1:T(8,128)}) %all-reduce.6.cloned.1.call-update) | async-done | bytes 1048592 | tf_op jit(solution)/shard_map/psum | solution.py:17
  488.2 1.6 copy.24
  489.7 1.4 fusion
  491.2 11.7 %cholesky.104 = f32[128,128]{1,0:T(8,128)S(1)} custom-call(f32[128,128]{1,0:T(8,128)S(1)} %cholesky.266), custom_call_target="Cholesky" | custom-call | tf_op jit(solution)/shard_map/jit(cholesky)/cholesky | solution.py:18
  502.9 0.1 cholesky.224
  503.1 9.8 %custom-call.27 = f32[1,128,128]{1,2,0:T(8,128)S(1)} custom-call(f32[1,128,128]{2,1,0:T(8,128)S(1)} %get-tuple-element.19), custom_call_target="InvertDiagBlocksLowerTriangular" | custom-call | tf_op jit(solution)/shard_map/jit(cholesky)/cholesky | solution.py:18
  512.9 0.3 constant_dynamic-update-slice_fusion.2
  513.2 0.3 convolution_subtract_fusion
  513.6 11.7 %cholesky.217 = f32[128,128]{1,0:T(8,128)S(1)} custom-call(f32[128,128]{1,0:T(8,128)S(1)} %cholesky.270), custom_call_target="Cholesky" | custom-call | tf_op jit(solution)/shard_map/jit(cholesky)/cholesky | solution.py:18
  525.3 10.0 %custom-call.28 = f32[1,128,128]{1,2,0:T(8,128)S(1)} custom-call(f32[1,128,128]{2,1,0:T(8,128)S(1)} %get-tuple-element.16), custom_call_target="InvertDiagBlocksLowerTriangular" | custom-call | tf_op jit(solution)/shard_map/jit(cholesky)/cholesky | solution.py:18
  535.3 0.3 convolution_dynamic-update-slice_fusion
  535.5 0.4 convolution_subtract_fusion.1
  535.9 11.7 %cholesky.238 = f32[128,128]{1,0:T(8,128)S(1)} custom-call(f32[128,128]{1,0:T(8,128)S(1)} %cholesky.275), custom_call_target="Cholesky" | custom-call | tf_op jit(solution)/shard_map/jit(cholesky)/cholesky | solution.py:18
  547.7 9.8 %custom-call.29 = f32[1,128,128]{1,2,0:T(8,128)S(1)} custom-call(f32[1,128,128]{2,1,0:T(8,128)S(1)} %get-tuple-element.13), custom_call_target="InvertDiagBlocksLowerTriangular" | custom-call | tf_op jit(solution)/shard_map/jit(cholesky)/cholesky | solution.py:18
  557.5 0.2 convolution_dynamic-update-slice_fusion.1
  557.7 0.4 convolution_subtract_fusion.2
  558.1 11.7 %cholesky.255 = f32[128,128]{1,0:T(8,128)S(1)} custom-call(f32[128,128]{1,0:T(8,128)S(1)} %convolution_subtract_fusion.2), custom_call_target="Cholesky" | custom-call | tf_op jit(solution)/shard_map/jit(cholesky)/cholesky | solution.py:18
  569.8 0.6 compare_reduce_fusion.1
  570.5 0.6 compare_reduce_fusion
  571.1 0.6 compare_reduce_fusion.2
  574.2 0.1 select_bitcast_fusion
  574.4 0.3 multiply_reduce_fusion
  574.7 0.9 fusion.7
  575.5 15.8 %fusion.1 = f32[256,4,8,128]{3,0,2,1:T(8,128)S(1)} fusion(f32[4,8,128,512]{3,2,1,0:T(8,128)} %bitcast.41, f32[512,512]{0,1:T(8,128)S(1)} %select_bitcast_fusion, f32[256]{0:T(256)S(1)} %sqrt.7), kind=kOutput, calls=%fused_computation.10 | convolution fusion | flops 6442582016 | bytes 13108224 | tf_op jit(solution)/shard_map/dot_general | solution.py:22
  591.3 4.4 copy.27
  (8 shorter events, 0.2 us)
Async XLA Ops:
  7.2 291.3 %all-reduce.4.cloned.1.call-start = ((), (), s32[]{:S(2)}) async-start(), calls=%async_computation.1 | async-start | bytes 2097152 | tf_op jit(solution)/shard_map/psum | solution.py:16
  250.8 237.3 %all-reduce.6.cloned.1.call-start = ((), (), s32[]{:S(2)}) async-start(), calls=%async_computation.2 | async-start | bytes 2097152 | tf_op jit(solution)/shard_map/psum | solution.py:17
Sparse Core Ops, SparseCore 0:
  251.0 47.4 all-reduce.3
  302.2 185.8 all-reduce.5
where the time goes:
time: 609 us; the launch traced here: 603 us
  waiting for transfers between devices  228 us (37%)
  blocking collectives  197 us (32%)
  other arithmetic  81.2 us (13%)
  local copies, waits for them, and re-layouts  44.5 us (7%)
  matrix products  34.9 us (6%)
  between operations  16.9 us (3%)
    all_to_all x1, blocking collectives, on_device(): lax.all_to_all(snapshot, 'wide', split_axis=2, concat_axis=0, tiled=True)  197 us
    psum x1, waiting for transfers between devices, on_device(): gram = lax.psum(gram, 'wide')  180 us
    another operation x14, other arithmetic, on_device(): upper = jnp.linalg.cholesky(gram).T  78.5 us
    psum x1, waiting for transfers between devices, on_device(): gram = lax.psum(gram, 'narrow')  47.5 us
    dot_general x1, matrix products, on_device(): jnp.dot(unfold, unfold.T, precision=lax.Precision.HIGHEST, preferred_elem...  17.2 us
    dot_general x1, matrix products, on_device(): jnp.dot(factor.T, unfold, precision=lax.Precision.HIGHEST, preferred_elem...  15.8 us
    unnamed x2, local copies, waits for them, and re-layouts  12.7 us
  transfers between devices with their start and end apart: 2, of which 2 were waited for; matrix products, arithmetic and copies ran while one was open for 2% of the time, Pallas kernels for 0%

commit v1 on v0

v1 whole, which is shorter than its diff:
```python
import functools

import jax
import jax.numpy as jnp
from jax import lax
from jax.experimental import pallas as pl
from jax.experimental.pallas import tpu as pltpu
from jax.sharding import PartitionSpec as P

RANK = 256
ROWS = 512
NZD, NXD, NCD, NYD = 8, 4, 2, 4
WIDE = NZD * NXD * NCD
CHUNKS = 8
MESH = pl.DeviceIdType.MESH
HIGHEST = lax.Precision.HIGHEST


def exchange_gram_kernel(
    x_ref, u_ref, g_ref,
    xin, stag, ubuf, gacc, r1, h2, r2, r3, gfull,
    in_sem, a_send, a_recv, out_sem, red_send, red_recv,
):
    w = lax.axis_index("wide")
    y = lax.axis_index("narrow")
    z, x, c = w // 8, (w // 2) % 4, w % 2
    piece = x * NYD + y

    def wide_id(zz, xx, cc):
        return zz * 8 + xx * 2 + cc

    barrier = pltpu.get_barrier_semaphore()

    def greet(i, carry):
        pl.semaphore_signal(barrier, inc=1, device_id=((w + i) % WIDE, y), device_id_type=MESH)
        return carry

    lax.fori_loop(1, WIDE, greet, 0)

    def greet_plane(i, carry):
        yy, xx = (y + 1 + i // NXD) % NYD, i % NXD
        pl.semaphore_signal(
            barrier, inc=1, device_id=(wide_id(z, xx, c), yy), device_id_type=MESH
        )
        return carry

    lax.fori_loop(0, (NYD - 1) * NXD, greet_plane, 0)

    def load(i, carry):
        yy, r = i // 8, i % 8
        pltpu.make_async_copy(
            x_ref.at[r, yy], xin.at[pl.ds(pl.multiple_of(i * 512, 512), 512)], in_sem.at[yy]
        ).start()
        return carry

    lax.fori_loop(0, 32, load, 0)

    def relayout(ch):
        yy, zh = ch // 2, ch % 2
        base = yy * 4096 + zh * 4

        def body(d, carry):
            for q in range(4):
                stag[ch, d, q] = xin[pl.ds(base + d * 8 + q, 8, stride=512), :]
            return carry

        lax.fori_loop(0, WIDE, body, 0, unroll=4)
        for q in range(4):
            ubuf[ch, q, w] = stag[ch, w, q]

    def wait_in(yy):
        whole = xin.at[pl.ds(pl.multiple_of(yy * 4096, 4096), 4096)]
        pltpu.make_async_copy(whole, whole, in_sem.at[yy]).wait()

    def send(ch):
        def body(i, carry):
            off = (i * 27) % WIDE
            t = wide_id((z + off // 8) % NZD, (x + (off // 2) % 4) % NXD, (c + off % 2) % NCD)
            pltpu.make_async_remote_copy(
                src_ref=stag.at[ch, t],
                dst_ref=ubuf.at[ch, :, w],
                send_sem=a_send.at[ch],
                recv_sem=a_recv.at[ch],
                device_id=(t, y),
                device_id_type=MESH,
            ).start()
            return carry

        lax.fori_loop(1, WIDE, body, 0)

    wait_in(0)
    relayout(0)
    pl.semaphore_wait(barrier, WIDE - 1 + (NYD - 1) * NXD)
    send(0)
    relayout(1)
    send(1)

    def send_two(yy, carry):
        wait_in(yy)
        for zh in range(2):
            relayout(yy * 2 + zh)
            send(yy * 2 + zh)
        return carry

    lax.fori_loop(1, 4, send_two, 0)

    gacc[...] = jnp.zeros_like(gacc)

    def gram(ch, carry):
        got = ubuf.at[ch, :, pl.ds(0, WIDE - 1)]
        pltpu.make_async_copy(got, got, a_recv.at[ch]).wait()
        pltpu.make_async_copy(ubuf.at[ch], u_ref.at[ch], out_sem.at[ch]).start()
        for q in range(0, 4, 2):
            left = ubuf[ch, q].reshape(ROWS, 128)
            right = ubuf[ch, q + 1].reshape(ROWS, 128)
            a = jnp.concatenate([left, right], axis=1)
            part = lax.dot_general(
                a, a[:RANK], (((1,), (1,)), ((), ())),
                precision=HIGHEST, preferred_element_type=jnp.float32,
            )
            gacc[...] += part.reshape(2, 16, 16, RANK)
        return carry

    lax.fori_loop(0, CHUNKS, gram, 0)

    partner = wide_id(z, x, 1 - c)
    pltpu.make_async_remote_copy(
        src_ref=gacc.at[1 - c], dst_ref=r1, send_sem=red_send.at[0], recv_sem=red_recv.at[0],
        device_id=(partner, y), device_id_type=MESH,
    ).start()
    pltpu.make_async_copy(r1, r1, red_recv.at[0]).wait()
    h2[...] = gacc[c] + r1[...]

    def plane(i, stage, source, target):
        t = (piece + i) % 16
        pltpu.make_async_remote_copy(
            src_ref=source(t), dst_ref=target, send_sem=red_send.at[stage],
            recv_sem=red_recv.at[stage], device_id=(wide_id(z, t // NYD, c), t % NYD),
            device_id_type=MESH,
        ).start()

    def scatter(i, carry):
        plane(i, 1, lambda t: h2.at[t], r2.at[piece])
        return carry

    lax.fori_loop(1, 16, scatter, 0)
    r2[piece] = h2[piece]
    got = r2.at[pl.ds(0, 15)]
    pltpu.make_async_copy(got, got, red_recv.at[1]).wait()
    total = r2[0]
    for i in range(1, 16):
        total = total + r2[i]
    r3[z] = total

    def along_z(i, carry):
        zz = (z + i) % NZD
        pltpu.make_async_remote_copy(
            src_ref=r3.at[z], dst_ref=r3.at[z], send_sem=red_send.at[2],
            recv_sem=red_recv.at[2], device_id=(wide_id(zz, x, c), y), device_id_type=MESH,
        ).start()
        return carry

    lax.fori_loop(1, NZD, along_z, 0)
    got = r3.at[pl.ds(0, NZD - 1)]
    pltpu.make_async_copy(got, got, red_recv.at[2]).wait()
    total = r3[0]
    for i in range(1, NZD):
        total = total + r3[i]
    gfull[c, piece] = total

    def gather(i, carry):
        plane(i, 3, lambda t: gfull.at[c, piece], gfull.at[c, piece])
        return carry

    lax.fori_loop(1, 16, gather, 0)
    got = gfull.at[c, pl.ds(0, 15)]
    pltpu.make_async_copy(got, got, red_recv.at[3]).wait()
    pltpu.make_async_remote_copy(
        src_ref=gfull.at[c], dst_ref=gfull.at[c], send_sem=red_send.at[4],
        recv_sem=red_recv.at[4], device_id=(partner, y), device_id_type=MESH,
    ).start()
    pltpu.make_async_copy(gfull.at[0], gfull.at[0], red_recv.at[4]).wait()
    g_ref[...] = gfull[...].reshape(ROWS, RANK)

    def drain(ch, carry):
        sent = stag.at[ch, pl.ds(0, WIDE - 1)]
        pltpu.make_async_copy(sent, sent, a_send.at[ch]).wait()
        pltpu.make_async_copy(ubuf.at[ch], u_ref.at[ch], out_sem.at[ch]).wait()
        return carry

    lax.fori_loop(0, CHUNKS, drain, 0)
    pltpu.make_async_copy(r1, r1, red_send.at[0]).wait()
    sent = h2.at[pl.ds(0, 15)]
    pltpu.make_async_copy(sent, sent, red_send.at[1]).wait()
    sent = r3.at[pl.ds(0, NZD - 1)]
    pltpu.make_async_copy(sent, sent, red_send.at[2]).wait()
    sent = gfull.at[c, pl.ds(0, 15)]
    pltpu.make_async_copy(sent, sent, red_send.at[3]).wait()
    pltpu.make_async_copy(gfull.at[0], gfull.at[0], red_send.at[4]).wait()


def exchange_gram(snapshot):
    f32 = jnp.float32
    dma = pltpu.SemaphoreType.DMA
    return pl.pallas_call(
        exchange_gram_kernel,
        name="exchange_gram",
        out_shape=(
            jax.ShapeDtypeStruct((CHUNKS, 4, WIDE, 8, 128), f32),
            jax.ShapeDtypeStruct((ROWS, RANK), f32),
        ),
        in_specs=[pl.BlockSpec(memory_space=pl.ANY)],
        out_specs=(
            pl.BlockSpec(memory_space=pl.ANY),
            pl.BlockSpec(memory_space=pltpu.VMEM),
        ),
        scratch_shapes=[
            pltpu.VMEM((4 * 8 * 512, 128), f32),
            pltpu.VMEM((CHUNKS, WIDE, 4, 8, 128), f32),
            pltpu.VMEM((CHUNKS, 4, WIDE, 8, 128), f32),
            pltpu.VMEM((2, 16, 16, RANK), f32),
            pltpu.VMEM((16, 16, RANK), f32),
            pltpu.VMEM((16, 16, RANK), f32),
            pltpu.VMEM((16, 16, RANK), f32),
            pltpu.VMEM((NZD, 16, RANK), f32),
            pltpu.VMEM((2, 16, 16, RANK), f32),
            dma((4,)), dma((CHUNKS,)), dma((CHUNKS,)), dma((CHUNKS,)), dma((5,)), dma((5,)),
        ],
        compiler_params=pltpu.CompilerParams(
            collective_id=0, has_side_effects=True, vmem_limit_bytes=48 << 20
        ),
    )(snapshot)


def core_kernel(u_ref, f_ref, core_ref):
    ft = f_ref[...]
    fh = ft.astype(jnp.bfloat16)
    fl = (ft - fh.astype(jnp.float32)).astype(jnp.bfloat16)
    dims = (((1,), (0,)), ((), ()))
    dot = functools.partial(lax.dot_general, dimension_numbers=dims, preferred_element_type=jnp.float32)
    for zz in range(0, 8, 2):
        a = jnp.concatenate(
            [u_ref[(zz + k) // 4, (zz + k) % 4].reshape(ROWS, 128) for k in range(2)], axis=1
        )
        ah = a.astype(jnp.bfloat16)
        al = (a - ah.astype(jnp.float32)).astype(jnp.bfloat16)
        out = dot(fh, ah) + (dot(fh, al) + dot(fl, ah))
        core_ref[:, 0, zz, :] = out[:, :128]
        core_ref[:, 0, zz + 1, :] = out[:, 128:]


def project(u, ft):
    f32 = jnp.float32
    return pl.pallas_call(
        core_kernel,
        name="project",
        grid=(4,),
        out_shape=jax.ShapeDtypeStruct((RANK, 4, 8, 128), f32),
        in_specs=[
            pl.BlockSpec((2, 4, WIDE, 8, 128), lambda i: (i, 0, 0, 0, 0)),
            pl.BlockSpec((RANK, ROWS), lambda i: (0, 0)),
        ],
        out_specs=pl.BlockSpec((RANK, 1, 8, 128), lambda i: (0, i, 0, 0)),
        compiler_params=pltpu.CompilerParams(vmem_limit_bytes=48 << 20),
    )(u, ft)


def on_device(snapshot):
    u, gram = exchange_gram(snapshot)
    low = jnp.linalg.cholesky(gram[:RANK])
    rows = lax.linalg.triangular_solve(low, gram.T, left_side=True, lower=True)
    rows = jnp.concatenate([low.T, rows[:, RANK:]], axis=1)
    lengths = jnp.sqrt(jnp.sum(rows * rows, axis=1))
    ft = rows / lengths[:, None]
    core = project(u, ft)
    return (core, ft.T)


def solution(mesh):
    in_specs = (P("wide", "narrow", None, None),)
    out_specs = (P(None, "narrow", "wide", None), P())
    return jax.shard_map(
        on_device, mesh=mesh, in_specs=in_specs, out_specs=out_specs, check_vma=False
    )
```

time: 609 us -> 292 us (0.48)
  Pallas kernels: 0 us -> 228 us
  waiting for transfers between devices: 228 us -> 0 us
  blocking collectives: 197 us -> 0 us
  local copies, waits for them, and re-layouts: 44.5 us -> 5.73 us
  matrix products: 34.9 us -> 1.9 us
  other arithmetic: 81.2 us -> 54.1 us
  between operations: 16.9 us -> 2.04 us
    psum x2 -> x0, waiting for transfers between devices: 228 us -> none  [the longest x1 180 us: on_device(): gram = lax.psum(gram, 'wide')]
    pallas_call x0 -> x2, Pallas kernels: none -> 228 us  [the longest x1 218 us: exchange_gram(): pl.pallas_call(exchange_gram_kernel, name='exchange_gram', out_shape=(jax...]
    all_to_all x1 -> x0, blocking collectives: 197 us -> none  [on_device(): lax.all_to_all(snapshot, 'wide', split_axis=2, concat_axis=0, tiled=True)]
    dot_general x2 -> x0, matrix products: 33 us -> none  [the longest x1 17.2 us: on_device(): jnp.dot(unfold, unfold.T, precision=lax.Precision.HIGHEST, preferred_elem...]
    another operation x14 -> x8, other arithmetic: 78.5 us -> 53.8 us  [the longest x6 33.9 us: on_device(): low = jnp.linalg.cholesky(gram[:RANK])]
    unnamed x2 -> x1, local copies, waits for them, and re-layouts: 12.7 us -> 0.99 us
    all_to_all x1 -> x0, local copies, waits for them, and re-layouts: 11.3 us -> none  [on_device(): lax.all_to_all(snapshot, 'wide', split_axis=2, concat_axis=0, tiled=True)]
    dot_general x1 -> x0, local copies, waits for them, and re-layouts: 9.4 us -> none  [on_device(): jnp.dot(factor.T, unfold, precision=lax.Precision.HIGHEST, preferred_elem...]
  transfers between devices with their start and end apart: 2 -> 0, of which waited for: 2 -> 0; matrix products, arithmetic and copies ran while one was open for 2% -> 0% of each run, Pallas kernels for 0% -> 0%
where the time goes in v1:
time: 292 us; the launch traced here: 291 us
  Pallas kernels  228 us (78%)
  other arithmetic  54.1 us (19%)
  local copies, waits for them, and re-layouts  5.73 us (2%)
    pallas_call x1, Pallas kernels, exchange_gram(): pl.pallas_call(exchange_gram_kernel, name='exchange_gram', out_shape=(jax...  218 us
    another operation x6, other arithmetic, on_device(): low = jnp.linalg.cholesky(gram[:RANK])  33.9 us
    another operation x2, other arithmetic, on_device(): rows = lax.linalg.triangular_solve(low, gram.T, left_side=True, lower=True)  19.9 us
    pallas_call x1, Pallas kernels, project(): pl.pallas_call(core_kernel, name='project', grid=(4,), out_shape=jax.Shap...  9.21 us

profile of v1, /device:TPU:1, one launch (start us, length us, event | category | flops | bytes accessed | tf_op | source)
XLA Modules:
  0.0 291.5 jit_solution(9041409984231959995)
XLA Ops:
  0.6 0.1 triangular_solve.42
  0.7 218.4 %exchange_gram.1 = (f32[8,4,64,8,128]{4,3,2,1,0:T(8,128)}, f32[512,256]{1,0:T(8,128)S(1)}) custom-call(f32[8,4,512,128]{3,2,1,0:T(8,128)} %x_ref.1), custom_call_target="tpu_custom_call" | custom-call | tf_op jit(solution)/shard_map/exchange_gram/pallas_call | solution.py:205
  219.1 0.2 copy.3
  219.4 0.1 copy.4
  219.6 11.7 %cholesky.50 = f32[128,128]{1,0:T(8,128)S(1)} custom-call(f32[128,128]{1,0:T(8,128)S(1)} %cholesky.118), custom_call_target="Cholesky" | custom-call | tf_op jit(solution)/shard_map/jit(cholesky)/cholesky | solution.py:270
  231.3 0.1 copy.5
  231.4 9.8 %custom-call.14 = f32[1,128,128]{1,2,0:T(8,128)S(1)} custom-call(f32[1,128,128]{2,1,0:T(8,128)S(1)} %get-tuple-element.33), custom_call_target="InvertDiagBlocksLowerTriangular" | custom-call | tf_op jit(solution)/shard_map/jit(cholesky)/cholesky | solution.py:270
  241.2 0.2 fusion.8
  241.4 0.3 convolution_subtract_fusion.1
  241.7 11.7 %cholesky.105 = f32[128,128]{1,0:T(8,128)S(1)} custom-call(f32[128,128]{1,0:T(8,128)S(1)} %convolution_subtract_fusion.1), custom_call_target="Cholesky" | custom-call | tf_op jit(solution)/shard_map/jit(cholesky)/cholesky | solution.py:270
  253.4 0.1 copy.6
  253.6 0.1 copy.7
  253.7 0.6 compare_reduce_fusion
  255.6 4.1 %while.1 = (s32[]{:T(128)}, f32[256,256]{0,1:T(8,128)S(1)}, s32[2,2]{1,0:T(2,128)S(1)}, f32[2,128,128]{2,1,0:T(8,128)S(1)}, s32[]{:T(128)}) while((s32[]{:T(128)}, f32[256,256]{0,1:T(8,128)S(1)}, s32[2,2]{1,0:T(2,128)S(1)}, f32[2,128,128]{2,1,0:T(8,128)S(1)}, s32[]{:T(128)}) %tuple.28), condition=%wide.while_cond, body=%wide.while_body.sunk | while | flops 2 | bytes 393329 | solution.py:271
  255.7 0.6 fusion.17
  256.2 1.3 dynamic-slice.7
  257.5 0.1 copy.12
  257.7 0.6 fusion.17
  258.3 1.3 dynamic-slice.7
  259.6 0.1 copy.12
  259.7 19.9 %custom-call.15 = f32[2,128,128]{1,2,0:T(8,128)S(1)} custom-call(f32[2,128,128]{2,1,0:T(8,128)S(1)} %get-tuple-element.13), custom_call_target="InvertDiagBlocksLowerTriangular" | custom-call | tf_op jit(solution)/shard_map/triangular_solve | solution.py:271
  279.6 0.4 fusion.1
  280.0 0.6 convolution_subtract_fusion
  280.6 0.4 fusion.7
  281.0 0.1 multiply_reduce_fusion
  281.2 0.1 broadcast_divide_fusion.f_ref
  281.3 9.2 %project.1 = f32[256,4,8,128]{3,2,1,0:T(8,128)} custom-call(f32[8,4,64,8,128]{4,3,2,1,0:T(8,128)} %get-tuple-element.4.u_ref, f32[256,512]{1,0:T(8,128)S(1)} %broadcast_divide_fusion.f_ref), custom_call_target="tpu_custom_call" | custom-call | tf_op jit(solution)/shard_map/project/pallas_call | solution.py:254
  290.5 1.0 copy.9
  (16 shorter events, 0.3 us)

commit v2 on v1

--- a/solution.py
+++ b/solution.py
@@ -115,10 +115,10 @@
             right = ubuf[ch, q + 1].reshape(ROWS, 128)
             a = jnp.concatenate([left, right], axis=1)
             part = lax.dot_general(
-                a, a[:RANK], (((1,), (1,)), ((), ())),
+                a[:RANK], a, (((1,), (1,)), ((), ())),
                 precision=HIGHEST, preferred_element_type=jnp.float32,
             )
-            gacc[...] += part.reshape(2, 16, 16, RANK)
+            gacc[...] += part.reshape(2, 16, 8, ROWS)
         return carry
 
     lax.fori_loop(0, CHUNKS, gram, 0)
@@ -180,7 +180,7 @@
         recv_sem=red_recv.at[4], device_id=(partner, y), device_id_type=MESH,
     ).start()
     pltpu.make_async_copy(gfull.at[0], gfull.at[0], red_recv.at[4]).wait()
-    g_ref[...] = gfull[...].reshape(ROWS, RANK)
+    g_ref[...] = gfull[...].reshape(RANK, ROWS)
 
     def drain(ch, carry):
         sent = stag.at[ch, pl.ds(0, WIDE - 1)]
@@ -207,7 +207,7 @@
         name="exchange_gram",
         out_shape=(
             jax.ShapeDtypeStruct((CHUNKS, 4, WIDE, 8, 128), f32),
-            jax.ShapeDtypeStruct((ROWS, RANK), f32),
+            jax.ShapeDtypeStruct((RANK, ROWS), f32),
         ),
         in_specs=[pl.BlockSpec(memory_space=pl.ANY)],
         out_specs=(
@@ -218,12 +218,12 @@
             pltpu.VMEM((4 * 8 * 512, 128), f32),
             pltpu.VMEM((CHUNKS, WIDE, 4, 8, 128), f32),
             pltpu.VMEM((CHUNKS, 4, WIDE, 8, 128), f32),
-            pltpu.VMEM((2, 16, 16, RANK), f32),
-            pltpu.VMEM((16, 16, RANK), f32),
-            pltpu.VMEM((16, 16, RANK), f32),
-            pltpu.VMEM((16, 16, RANK), f32),
-            pltpu.VMEM((NZD, 16, RANK), f32),
-            pltpu.VMEM((2, 16, 16, RANK), f32),
+            pltpu.VMEM((2, 16, 8, ROWS), f32),
+            pltpu.VMEM((16, 8, ROWS), f32),
+            pltpu.VMEM((16, 8, ROWS), f32),
+            pltpu.VMEM((16, 8, ROWS), f32),
+            pltpu.VMEM((NZD, 8, ROWS), f32),
+            pltpu.VMEM((2, 16, 8, ROWS), f32),
             dma((4,)), dma((CHUNKS,)), dma((CHUNKS,)), dma((CHUNKS,)), dma((5,)), dma((5,)),
         ],
         compiler_params=pltpu.CompilerParams(
@@ -232,48 +232,152 @@
     )(snapshot)
 
 
-def core_kernel(u_ref, f_ref, core_ref):
-    ft = f_ref[...]
-    fh = ft.astype(jnp.bfloat16)
-    fl = (ft - fh.astype(jnp.float32)).astype(jnp.bfloat16)
-    dims = (((1,), (0,)), ((), ()))
-    dot = functools.partial(lax.dot_general, dimension_numbers=dims, preferred_element_type=jnp.float32)
+def unit_lower_inverse(rows):
+    tile = (8, 128)
+    lane = lax.broadcasted_iota(jnp.int32, tile, 1)
+    sub = lax.broadcasted_iota(jnp.int32, tile, 0)
+    rows, done = list(rows), []
+
+    def lanes(v, k):
+        return jnp.broadcast_to(v[:, k : k + 1], tile)
+
+    def subs(v, k):
+        return jnp.broadcast_to(v[k : k + 1, :], tile)
+
+    for g in range(16):
+        v = rows[g]
+        inside = (lane >= 8 * g) & (lane < 8 * g + 8)
+        cols = [lanes(v, 8 * g + k) for k in range(8)]
+        a = [[subs(cols[k], i) if i >= k else None for k in range(8)] for i in range(8)]
+        n = [[None] * 8 for _ in range(8)]
+        m = [[None] * 8 for _ in range(8)]
+        inv = [None] * 8
+        for k in range(8):
+            inv[k] = 1.0 / a[k][k]
+            for i in range(k + 1, 8):
+                m[i][k] = a[i][k] * inv[k]
+                for j in range(k + 1, i + 1):
+                    a[i][j] = a[i][j] - m[i][k] * a[j][k]
+        for j in range(8):
+            for i in range(j + 1, 8):
+                s = m[i][j]
+                for t in range(j + 1, i):
+                    s = s + m[i][t] * n[t][j]
+                n[i][j] = -s
+        vt = jnp.where(inside, jnp.where(lane == 8 * g + sub, 1.0, 0.0), v)
+        p = vt
+        for k in range(7):
+            col = jnp.zeros(tile, jnp.float32)
+            for i in range(k + 1, 8):
+                col = jnp.where(sub == i, n[i][k], col)
+            p = p + col * subs(vt, k)
+        scale = inv[0]
+        for i in range(1, 8):
+            scale = jnp.where(sub == i, inv[i], scale)
+        q = p * scale
+        qb = [subs(q, i) for i in range(8)]
+        tb = []
+        for j in range(8):
+            s = qb[j]
+            for i in range(j + 1, 8):
+                s = s + n[i][j] * qb[i]
+            tb.append(s)
+        done.append(jnp.where(lane < 8 * g + 8, p, 0.0))
+        for i in range(g + 1, 16):
+            vi = rows[i]
+            c = [lanes(vi, 8 * g + k) for k in range(8)]
+            vi = jnp.where(inside, 0.0, vi)
+            s0 = c[0] * tb[0]
+            s1 = c[1] * tb[1]
+            for k in range(2, 8, 2):
+                s0 = s0 + c[k] * tb[k]
+                s1 = s1 + c[k + 1] * tb[k + 1]
+            rows[i] = vi - (s0 + s1)
+    return done
+
+
+def eliminate(a):
+    n = a.shape[1]
+    inv = jnp.concatenate(unit_lower_inverse([a[8 * g : 8 * g + 8, :128] for g in range(16)]), axis=0)
+    s = jnp.dot(inv, a, precision=HIGHEST, preferred_element_type=jnp.float32)
+    row = lax.broadcasted_iota(jnp.int32, (128, n), 0)
+    lane = lax.broadcasted_iota(jnp.int32, (128, n), 1)
+    s = jnp.where(lane >= row, s, 0.0)
+    d = jnp.sum(jnp.where(lane[:, :128] == row[:, :128], s[:, :128], 0.0), axis=1, keepdims=True)
+    return s, d
+
+
+def unit_rows(s, d):
+    r = s * (1.0 / jnp.sqrt(d))
+    return r * (1.0 / jnp.sqrt(jnp.sum(r * r, axis=1, keepdims=True)))
+
+
+def factor_rows(g_ref, ft_ref):
+    s1, d1 = eliminate(g_ref[:128, :])
+    ft_ref[:128, :] = unit_rows(s1, d1)
+    right = s1[:, 128:]
+    schur = lax.dot_general(right[:, :128] * (1.0 / d1), right, (((0,), (0,)), ((), ())),
+        precision=HIGHEST, preferred_element_type=jnp.float32)
+    s2, d2 = eliminate(g_ref[128:, 128:] - schur)
+    ft_ref[128:, :128] = jnp.zeros((128, 128), jnp.float32)
+    ft_ref[128:, 128:] = unit_rows(s2, d2)
+
+
+def split(v):
+    high = v.astype(jnp.bfloat16)
+    return high, (v - high.astype(jnp.float32)).astype(jnp.bfloat16)
+
+
+def core_kernel(u_ref, g_ref, core_ref, factor_ref, ft, fh, fl):
+    i = pl.program_id(0)
+
+    @pl.when(i == 0)
+    def _():
+        factor_rows(g_ref, ft)
+        fh[...], fl[...] = split(ft[...])
+
+    factor_ref[...] = ft[:, pl.ds(pl.multiple_of(i * 128, 128), 128)].T
+    high, low = fh[...], fl[...]
+    dot = functools.partial(jnp.dot, preferred_element_type=jnp.float32)
+    flat = core_ref.reshape(RANK * 8, 128)
     for zz in range(0, 8, 2):
-        a = jnp.concatenate(
-            [u_ref[(zz + k) // 4, (zz + k) % 4].reshape(ROWS, 128) for k in range(2)], axis=1
-        )
-        ah = a.astype(jnp.bfloat16)
-        al = (a - ah.astype(jnp.float32)).astype(jnp.bfloat16)
-        out = dot(fh, ah) + (dot(fh, al) + dot(fl, ah))
-        core_ref[:, 0, zz, :] = out[:, :128]
-        core_ref[:, 0, zz + 1, :] = out[:, 128:]
-
-
-def project(u, ft):
+        cells = [u_ref[(zz + k) // 4, (zz + k) % 4].reshape(ROWS, 128) for k in range(2)]
+        ah, al = split(jnp.concatenate(cells, axis=1))
+        out = dot(high, ah) + (dot(high, al) + dot(low, ah))
+        for k in range(2):
+            flat[pl.ds(zz + k, RANK, stride=8), :] = out[:, 128 * k : 128 * k + 128]
+
+
+def project(u, gram):
     f32 = jnp.float32
     return pl.pallas_call(
         core_kernel,
         name="project",
-        grid=(4,),
-        out_shape=jax.ShapeDtypeStruct((RANK, 4, 8, 128), f32),
+        grid=(NYD,),
+        out_shape=(
+            jax.ShapeDtypeStruct((RANK, NYD, 8, 128), f32),
+            jax.ShapeDtypeStruct((ROWS, RANK), f32),
+        ),
         in_specs=[
             pl.BlockSpec((2, 4, WIDE, 8, 128), lambda i: (i, 0, 0, 0, 0)),
             pl.BlockSpec((RANK, ROWS), lambda i: (0, 0)),
         ],
-        out_specs=pl.BlockSpec((RANK, 1, 8, 128), lambda i: (0, i, 0, 0)),
+        out_specs=(
+            pl.BlockSpec((RANK, 1, 8, 128), lambda i: (0, i, 0, 0)),
+            pl.BlockSpec((128, RANK), lambda i: (i, 0)),
+        ),
+        scratch_shapes=[
+            pltpu.VMEM((RANK, ROWS), f32),
+            pltpu.VMEM((RANK, ROWS), jnp.bfloat16),
+            pltpu.VMEM((RANK, ROWS), jnp.bfloat16),
+        ],
         compiler_params=pltpu.CompilerParams(vmem_limit_bytes=48 << 20),
-    )(u, ft)
+    )(u, gram)
 
 
 def on_device(snapshot):
     u, gram = exchange_gram(snapshot)
-    low = jnp.linalg.cholesky(gram[:RANK])
-    rows = lax.linalg.triangular_solve(low, gram.T, left_side=True, lower=True)
-    rows = jnp.concatenate([low.T, rows[:, RANK:]], axis=1)
-    lengths = jnp.sqrt(jnp.sum(rows * rows, axis=1))
-    ft = rows / lengths[:, None]
-    core = project(u, ft)
-    return (core, ft.T)
+    return project(u, gram)
 
 
 def solution(mesh):

time: 292 us -> 239 us (0.82)
  other arithmetic: 54.1 us -> 0 us
  Pallas kernels: 228 us -> 238 us
  local copies, waits for them, and re-layouts: 5.73 us -> 0 us
    another operation x8 -> x0, other arithmetic: 53.8 us -> none  [the longest x6 33.9 us: on_device(): low = jnp.linalg.cholesky(gram[:RANK])]
    pallas_call x1, Pallas kernels: 9.21 us -> 19.5 us  [project(): pl.pallas_call(core_kernel, name='project', grid=(NYD,), out_shape=(jax.S...]
    another operation x18 -> x0, local copies, waits for them, and re-layouts: 4.39 us -> none
where the time goes in v2:
time: 239 us
  Pallas kernels  238 us (100%)
    pallas_call x1, Pallas kernels, exchange_gram(): pl.pallas_call(exchange_gram_kernel, name='exchange_gram', out_shape=(jax...  218 us
    pallas_call x1, Pallas kernels, project(): pl.pallas_call(core_kernel, name='project', grid=(NYD,), out_shape=(jax.S...  19.5 us

profile of v2, /device:TPU:1, one launch (start us, length us, event | category | flops | bytes accessed | tf_op | source)
XLA Modules:
  0.0 238.6 jit_solution(11015188026701658017)
XLA Ops:
  0.6 218.5 %exchange_gram.1 = (f32[8,4,64,8,128]{4,3,2,1,0:T(8,128)}, f32[256,512]{1,0:T(8,128)S(1)}) custom-call(f32[8,4,512,128]{3,2,1,0:T(8,128)} %x_ref.1), custom_call_target="tpu_custom_call" | custom-call | tf_op jit(solution)/shard_map/exchange_gram/pallas_call | solution.py:205
  219.1 19.5 %project.1 = (f32[256,4,8,128]{3,2,1,0:T(8,128)}, f32[512,256]{1,0:T(8,128)}) custom-call(f32[8,4,64,8,128]{4,3,2,1,0:T(8,128)} %get-tuple-element.4.u_ref, f32[256,512]{1,0:T(8,128)S(1)} %get-tuple-element.5.g_ref), custom_call_target="tpu_custom_call" | custom-call | tf_op jit(solution)/shard_map/project/pallas_call | solution.py:353

commit v3 on v2

--- a/solution.py
+++ b/solution.py
@@ -232,7 +232,13 @@
     )(snapshot)
 
 
-def unit_lower_inverse(rows):
+def tree(terms):
+    while len(terms) > 1:
+        terms = [sum(terms[i + 1 : i + 2], terms[i]) for i in range(0, len(terms), 2)]
+    return terms[0]
+
+
+def unit_lower_inverse(rows, tmp):
     tile = (8, 128)
     lane = lax.broadcasted_iota(jnp.int32, tile, 1)
     sub = lax.broadcasted_iota(jnp.int32, tile, 0)
@@ -248,7 +254,12 @@
         v = rows[g]
         inside = (lane >= 8 * g) & (lane < 8 * g + 8)
         cols = [lanes(v, 8 * g + k) for k in range(8)]
-        a = [[subs(cols[k], i) if i >= k else None for k in range(8)] for i in range(8)]
+        base = 256 * (g % 2)
+        for k in range(8):
+            tmp[base + 8 * k : base + 8 * k + 8, :] = cols[k]
+        def row(r):
+            return tmp[pl.ds(base + r, 8, stride=0), :]
+        a = [[row(8 * k + i) if i >= k else None for k in range(8)] for i in range(8)]
         n = [[None] * 8 for _ in range(8)]
         m = [[None] * 8 for _ in range(8)]
         inv = [None] * 8
@@ -265,40 +276,35 @@
                     s = s + m[i][t] * n[t][j]
                 n[i][j] = -s
         vt = jnp.where(inside, jnp.where(lane == 8 * g + sub, 1.0, 0.0), v)
-        p = vt
+        tmp[base + 64 : base + 72, :] = vt
+        terms = [vt]
         for k in range(7):
             col = jnp.zeros(tile, jnp.float32)
             for i in range(k + 1, 8):
                 col = jnp.where(sub == i, n[i][k], col)
-            p = p + col * subs(vt, k)
+            terms.append(col * row(64 + k))
+        p = tree(terms)
         scale = inv[0]
         for i in range(1, 8):
             scale = jnp.where(sub == i, inv[i], scale)
         q = p * scale
-        qb = [subs(q, i) for i in range(8)]
+        tmp[base + 72 : base + 80, :] = q
+        qb = [row(72 + i) for i in range(8)]
         tb = []
         for j in range(8):
-            s = qb[j]
-            for i in range(j + 1, 8):
-                s = s + n[i][j] * qb[i]
-            tb.append(s)
+            tb.append(tree([qb[j]] + [n[i][j] * qb[i] for i in range(j + 1, 8)]))
         done.append(jnp.where(lane < 8 * g + 8, p, 0.0))
         for i in range(g + 1, 16):
             vi = rows[i]
             c = [lanes(vi, 8 * g + k) for k in range(8)]
             vi = jnp.where(inside, 0.0, vi)
-            s0 = c[0] * tb[0]
-            s1 = c[1] * tb[1]
-            for k in range(2, 8, 2):
-                s0 = s0 + c[k] * tb[k]
-                s1 = s1 + c[k + 1] * tb[k + 1]
-            rows[i] = vi - (s0 + s1)
+            rows[i] = vi - tree([c[k] * tb[k] for k in range(8)])
     return done
 
 
-def eliminate(a):
+def eliminate(a, tmp):
     n = a.shape[1]
-    inv = jnp.concatenate(unit_lower_inverse([a[8 * g : 8 * g + 8, :128] for g in range(16)]), axis=0)
+    inv = jnp.concatenate(unit_lower_inverse([a[8 * g : 8 * g + 8, :128] for g in range(16)], tmp), axis=0)
     s = jnp.dot(inv, a, precision=HIGHEST, preferred_element_type=jnp.float32)
     row = lax.broadcasted_iota(jnp.int32, (128, n), 0)
     lane = lax.broadcasted_iota(jnp.int32, (128, n), 1)
@@ -312,13 +318,13 @@
     return r * (1.0 / jnp.sqrt(jnp.sum(r * r, axis=1, keepdims=True)))
 
 
-def factor_rows(g_ref, ft_ref):
-    s1, d1 = eliminate(g_ref[:128, :])
+def factor_rows(g_ref, ft_ref, tmp):
+    s1, d1 = eliminate(g_ref[:128, :], tmp)
     ft_ref[:128, :] = unit_rows(s1, d1)
     right = s1[:, 128:]
     schur = lax.dot_general(right[:, :128] * (1.0 / d1), right, (((0,), (0,)), ((), ())),
         precision=HIGHEST, preferred_element_type=jnp.float32)
-    s2, d2 = eliminate(g_ref[128:, 128:] - schur)
+    s2, d2 = eliminate(g_ref[128:, 128:] - schur, tmp)
     ft_ref[128:, :128] = jnp.zeros((128, 128), jnp.float32)
     ft_ref[128:, 128:] = unit_rows(s2, d2)
 
@@ -328,24 +334,34 @@
     return high, (v - high.astype(jnp.float32)).astype(jnp.bfloat16)
 
 
-def core_kernel(u_ref, g_ref, core_ref, factor_ref, ft, fh, fl):
-    i = pl.program_id(0)
-
-    @pl.when(i == 0)
-    def _():
-        factor_rows(g_ref, ft)
-        fh[...], fl[...] = split(ft[...])
-
-    factor_ref[...] = ft[:, pl.ds(pl.multiple_of(i * 128, 128), 128)].T
-    high, low = fh[...], fl[...]
+def core_kernel(u_ref, g_ref, core_ref, factor_ref, ubuf, cbuf, ft, tmp, in_sem, out_sem):
+    def begin(ch, carry):
+        pltpu.make_async_copy(u_ref.at[ch], ubuf.at[ch], in_sem.at[ch]).start()
+        return carry
+
+    lax.fori_loop(0, CHUNKS, begin, 0)
+    factor_rows(g_ref, ft, tmp)
+    high, low = split(ft[...])
     dot = functools.partial(jnp.dot, preferred_element_type=jnp.float32)
-    flat = core_ref.reshape(RANK * 8, 128)
-    for zz in range(0, 8, 2):
-        cells = [u_ref[(zz + k) // 4, (zz + k) % 4].reshape(ROWS, 128) for k in range(2)]
-        ah, al = split(jnp.concatenate(cells, axis=1))
-        out = dot(high, ah) + (dot(high, al) + dot(low, ah))
-        for k in range(2):
-            flat[pl.ds(zz + k, RANK, stride=8), :] = out[:, 128 * k : 128 * k + 128]
+    flat = cbuf.reshape(NYD * RANK * 8, 128)
+
+    def end(ch, carry):
+        pltpu.make_async_copy(u_ref.at[ch], ubuf.at[ch], in_sem.at[ch]).wait()
+        return carry
+
+    lax.fori_loop(0, CHUNKS, end, 0)
+    for y in range(NYD):
+        for zz in range(0, 8, 2):
+            cells = [ubuf[2 * y + (zz + k) // 4, (zz + k) % 4].reshape(ROWS, 128) for k in range(2)]
+            ah, al = split(jnp.concatenate(cells, axis=1))
+            out = dot(high, ah) + (dot(high, al) + dot(low, ah))
+            for k in range(2):
+                start = y * RANK * 8 + zz + k
+                flat[pl.ds(start, RANK, stride=8), :] = out[:, 128 * k : 128 * k + 128]
+        pltpu.make_async_copy(cbuf.at[y], core_ref.at[:, y], out_sem.at[y]).start()
+        factor_ref[128 * y : 128 * y + 128, :] = ft[:, 128 * y : 128 * y + 128].T
+    for y in range(NYD):
+        pltpu.make_async_copy(cbuf.at[y], core_ref.at[:, y], out_sem.at[y]).wait()
 
 
 def project(u, gram):
@@ -353,23 +369,19 @@
     return pl.pallas_call(
         core_kernel,
         name="project",
-        grid=(NYD,),
         out_shape=(
             jax.ShapeDtypeStruct((RANK, NYD, 8, 128), f32),
             jax.ShapeDtypeStruct((ROWS, RANK), f32),
         ),
-        in_specs=[
-            pl.BlockSpec((2, 4, WIDE, 8, 128), lambda i: (i, 0, 0, 0, 0)),
-            pl.BlockSpec((RANK, ROWS), lambda i: (0, 0)),
-        ],
-        out_specs=(
-            pl.BlockSpec((RANK, 1, 8, 128), lambda i: (0, i, 0, 0)),
-            pl.BlockSpec((128, RANK), lambda i: (i, 0)),
-        ),
+        in_specs=[pl.BlockSpec(memory_space=pl.ANY), pl.BlockSpec(memory_space=pltpu.VMEM)],
+        out_specs=(pl.BlockSpec(memory_space=pl.ANY), pl.BlockSpec(memory_space=pltpu.VMEM)),
         scratch_shapes=[
+            pltpu.VMEM((CHUNKS, 4, WIDE, 8, 128), f32),
+            pltpu.VMEM((NYD, RANK, 8, 128), f32),
             pltpu.VMEM((RANK, ROWS), f32),
-            pltpu.VMEM((RANK, ROWS), jnp.bfloat16),
-            pltpu.VMEM((RANK, ROWS), jnp.bfloat16),
+            pltpu.VMEM((512, 128), f32),
+            pltpu.SemaphoreType.DMA((CHUNKS,)),
+            pltpu.SemaphoreType.DMA((NYD,)),
         ],
         compiler_params=pltpu.CompilerParams(vmem_limit_bytes=48 << 20),
     )(u, gram)

time: 239 us -> 235 us (0.983)
  Pallas kernels: 238 us -> 234 us
    pallas_call x1, Pallas kernels: 19.5 us -> 15.7 us  [project(): pl.pallas_call(core_kernel, name='project', out_shape=(jax.ShapeDtypeStru...]
where the time goes in v3:
time: 235 us
  Pallas kernels  234 us (100%)
    pallas_call x1, Pallas kernels, exchange_gram(): pl.pallas_call(exchange_gram_kernel, name='exchange_gram', out_shape=(jax...  218 us
    pallas_call x1, Pallas kernels, project(): pl.pallas_call(core_kernel, name='project', out_shape=(jax.ShapeDtypeStru...  15.7 us

profile of v3, /device:TPU:1, one launch (start us, length us, event | category | flops | bytes accessed | tf_op | source)
XLA Modules:
  0.0 234.8 jit_solution(2957476035021110064)
XLA Ops:
  0.6 218.5 %exchange_gram.1 = (f32[8,4,64,8,128]{4,3,2,1,0:T(8,128)}, f32[256,512]{1,0:T(8,128)S(1)}) custom-call(f32[8,4,512,128]{3,2,1,0:T(8,128)} %x_ref.1), custom_call_target="tpu_custom_call" | custom-call | tf_op jit(solution)/shard_map/exchange_gram/pallas_call | solution.py:205
  219.1 15.7 %project.1 = (f32[256,4,8,128]{3,2,1,0:T(8,128)}, f32[512,256]{1,0:T(8,128)}) custom-call(f32[8,4,64,8,128]{4,3,2,1,0:T(8,128)} %get-tuple-element.4.u_ref, f32[256,512]{1,0:T(8,128)S(1)} %get-tuple-element.5.g_ref), custom_call_target="tpu_custom_call" | custom-call | tf_op jit(solution)/shard_map/project/pallas_call | solution.py:369

commit v4 on v3

--- a/solution.py
+++ b/solution.py
@@ -12,14 +12,23 @@
 NZD, NXD, NCD, NYD = 8, 4, 2, 4
 WIDE = NZD * NXD * NCD
 CHUNKS = 8
+PLANE = (
+    (2, 2), (2, 1), (2, 3), (1, 2), (3, 2), (1, 1), (1, 3), (3, 1),
+    (3, 3), (0, 2), (2, 0), (0, 1), (0, 3), (1, 0), (3, 0),
+)
 MESH = pl.DeviceIdType.MESH
 HIGHEST = lax.Precision.HIGHEST
 
 
+def split(v):
+    high = v.astype(jnp.bfloat16)
+    return high, (v - high.astype(jnp.float32)).astype(jnp.bfloat16)
+
+
 def exchange_gram_kernel(
-    x_ref, u_ref, g_ref,
-    xin, stag, ubuf, gacc, r1, h2, r2, r3, gfull,
-    in_sem, a_send, a_recv, out_sem, red_send, red_recv,
+    x_ref, uh_ref, ul_ref, g_ref,
+    xin, stag, ubuf, uh, ul, gacc, r1, h2, r2, r3, gfull,
+    in_sem, a_send, a_recv, out_sem, red_send, red_recv, piece_recv,
 ):
     w = lax.axis_index("wide")
     y = lax.axis_index("narrow")
@@ -109,7 +118,6 @@
     def gram(ch, carry):
         got = ubuf.at[ch, :, pl.ds(0, WIDE - 1)]
         pltpu.make_async_copy(got, got, a_recv.at[ch]).wait()
-        pltpu.make_async_copy(ubuf.at[ch], u_ref.at[ch], out_sem.at[ch]).start()
         for q in range(0, 4, 2):
             left = ubuf[ch, q].reshape(ROWS, 128)
             right = ubuf[ch, q + 1].reshape(ROWS, 128)
@@ -119,6 +127,12 @@
                 precision=HIGHEST, preferred_element_type=jnp.float32,
             )
             gacc[...] += part.reshape(2, 16, 8, ROWS)
+            high, low = split(a)
+            for k in range(2):
+                uh[ch, q + k] = high[:, 128 * k : 128 * k + 128]
+                ul[ch, q + k] = low[:, 128 * k : 128 * k + 128]
+        pltpu.make_async_copy(uh.at[ch], uh_ref.at[ch], out_sem.at[0, ch]).start()
+        pltpu.make_async_copy(ul.at[ch], ul_ref.at[ch], out_sem.at[1, ch]).start()
         return carry
 
     lax.fori_loop(0, CHUNKS, gram, 0)
@@ -131,19 +145,12 @@
     pltpu.make_async_copy(r1, r1, red_recv.at[0]).wait()
     h2[...] = gacc[c] + r1[...]
 
-    def plane(i, stage, source, target):
-        t = (piece + i) % 16
+    for dx, dy in PLANE:
+        xx, yy = (x + dx) % NXD, (y + dy) % NYD
         pltpu.make_async_remote_copy(
-            src_ref=source(t), dst_ref=target, send_sem=red_send.at[stage],
-            recv_sem=red_recv.at[stage], device_id=(wide_id(z, t // NYD, c), t % NYD),
-            device_id_type=MESH,
+            src_ref=h2.at[xx * NYD + yy], dst_ref=r2.at[piece], send_sem=red_send.at[1],
+            recv_sem=red_recv.at[1], device_id=(wide_id(z, xx, c), yy), device_id_type=MESH,
         ).start()
-
-    def scatter(i, carry):
-        plane(i, 1, lambda t: h2.at[t], r2.at[piece])
-        return carry
-
-    lax.fori_loop(1, 16, scatter, 0)
     r2[piece] = h2[piece]
     got = r2.at[pl.ds(0, 15)]
     pltpu.make_async_copy(got, got, red_recv.at[1]).wait()
@@ -168,24 +175,31 @@
         total = total + r3[i]
     gfull[c, piece] = total
 
-    def gather(i, carry):
-        plane(i, 3, lambda t: gfull.at[c, piece], gfull.at[c, piece])
-        return carry
-
-    lax.fori_loop(1, 16, gather, 0)
-    got = gfull.at[c, pl.ds(0, 15)]
-    pltpu.make_async_copy(got, got, red_recv.at[3]).wait()
-    pltpu.make_async_remote_copy(
-        src_ref=gfull.at[c], dst_ref=gfull.at[c], send_sem=red_send.at[4],
-        recv_sem=red_recv.at[4], device_id=(partner, y), device_id_type=MESH,
-    ).start()
-    pltpu.make_async_copy(gfull.at[0], gfull.at[0], red_recv.at[4]).wait()
+    def across(p):
+        pltpu.make_async_remote_copy(
+            src_ref=gfull.at[c, p], dst_ref=gfull.at[c, p], send_sem=red_send.at[4],
+            recv_sem=red_recv.at[3], device_id=(partner, y), device_id_type=MESH,
+        ).start()
+
+    for dx, dy in PLANE:
+        xx, yy = (x + dx) % NXD, (y + dy) % NYD
+        pltpu.make_async_remote_copy(
+            src_ref=gfull.at[c, piece], dst_ref=gfull.at[c, piece], send_sem=red_send.at[3],
+            recv_sem=piece_recv.at[piece], device_id=(wide_id(z, xx, c), yy), device_id_type=MESH,
+        ).start()
+    across(piece)
+    for dx, dy in PLANE[::-1]:
+        p = ((x + NXD - dx) % NXD) * NYD + (y + NYD - dy) % NYD
+        pltpu.make_async_copy(gfull.at[c, p], gfull.at[c, p], piece_recv.at[p]).wait()
+        across(p)
+    pltpu.make_async_copy(gfull.at[0], gfull.at[0], red_recv.at[3]).wait()
     g_ref[...] = gfull[...].reshape(RANK, ROWS)
 
     def drain(ch, carry):
         sent = stag.at[ch, pl.ds(0, WIDE - 1)]
         pltpu.make_async_copy(sent, sent, a_send.at[ch]).wait()
-        pltpu.make_async_copy(ubuf.at[ch], u_ref.at[ch], out_sem.at[ch]).wait()
+        pltpu.make_async_copy(uh.at[ch], uh_ref.at[ch], out_sem.at[0, ch]).wait()
+        pltpu.make_async_copy(ul.at[ch], ul_ref.at[ch], out_sem.at[1, ch]).wait()
         return carry
 
     lax.fori_loop(0, CHUNKS, drain, 0)
@@ -206,11 +220,13 @@
         exchange_gram_kernel,
         name="exchange_gram",
         out_shape=(
-            jax.ShapeDtypeStruct((CHUNKS, 4, WIDE, 8, 128), f32),
+            jax.ShapeDtypeStruct((CHUNKS, 4, ROWS, 128), jnp.bfloat16),
+            jax.ShapeDtypeStruct((CHUNKS, 4, ROWS, 128), jnp.bfloat16),
             jax.ShapeDtypeStruct((RANK, ROWS), f32),
         ),
         in_specs=[pl.BlockSpec(memory_space=pl.ANY)],
         out_specs=(
+            pl.BlockSpec(memory_space=pl.ANY),
             pl.BlockSpec(memory_space=pl.ANY),
             pl.BlockSpec(memory_space=pltpu.VMEM),
         ),
@@ -218,13 +234,15 @@
             pltpu.VMEM((4 * 8 * 512, 128), f32),
             pltpu.VMEM((CHUNKS, WIDE, 4, 8, 128), f32),
             pltpu.VMEM((CHUNKS, 4, WIDE, 8, 128), f32),
+            pltpu.VMEM((CHUNKS, 4, ROWS, 128), jnp.bfloat16),
+            pltpu.VMEM((CHUNKS, 4, ROWS, 128), jnp.bfloat16),
             pltpu.VMEM((2, 16, 8, ROWS), f32),
             pltpu.VMEM((16, 8, ROWS), f32),
             pltpu.VMEM((16, 8, ROWS), f32),
             pltpu.VMEM((16, 8, ROWS), f32),
             pltpu.VMEM((NZD, 8, ROWS), f32),
             pltpu.VMEM((2, 16, 8, ROWS), f32),
-            dma((4,)), dma((CHUNKS,)), dma((CHUNKS,)), dma((CHUNKS,)), dma((5,)), dma((5,)),
+            dma((4,)), dma((CHUNKS,)), dma((CHUNKS,)), dma((2, CHUNKS)), dma((5,)), dma((4,)), dma((16,)),
         ],
         compiler_params=pltpu.CompilerParams(
             collective_id=0, has_side_effects=True, vmem_limit_bytes=48 << 20
@@ -329,14 +347,12 @@
     ft_ref[128:, 128:] = unit_rows(s2, d2)
 
 
-def split(v):
-    high = v.astype(jnp.bfloat16)
-    return high, (v - high.astype(jnp.float32)).astype(jnp.bfloat16)
-
-
-def core_kernel(u_ref, g_ref, core_ref, factor_ref, ubuf, cbuf, ft, tmp, in_sem, out_sem):
+def core_kernel(
+    uh_ref, ul_ref, g_ref, core_ref, factor_ref, uh, ul, cbuf, ft, tmp, in_sem, out_sem
+):
     def begin(ch, carry):
-        pltpu.make_async_copy(u_ref.at[ch], ubuf.at[ch], in_sem.at[ch]).start()
+        pltpu.make_async_copy(uh_ref.at[ch], uh.at[ch], in_sem.at[0, ch]).start()
+        pltpu.make_async_copy(ul_ref.at[ch], ul.at[ch], in_sem.at[1, ch]).start()
         return carry
 
     lax.fori_loop(0, CHUNKS, begin, 0)
@@ -346,14 +362,16 @@
     flat = cbuf.reshape(NYD * RANK * 8, 128)
 
     def end(ch, carry):
-        pltpu.make_async_copy(u_ref.at[ch], ubuf.at[ch], in_sem.at[ch]).wait()
+        pltpu.make_async_copy(uh_ref.at[ch], uh.at[ch], in_sem.at[0, ch]).wait()
+        pltpu.make_async_copy(ul_ref.at[ch], ul.at[ch], in_sem.at[1, ch]).wait()
         return carry
 
     lax.fori_loop(0, CHUNKS, end, 0)
     for y in range(NYD):
         for zz in range(0, 8, 2):
-            cells = [ubuf[2 * y + (zz + k) // 4, (zz + k) % 4].reshape(ROWS, 128) for k in range(2)]
-            ah, al = split(jnp.concatenate(cells, axis=1))
+            ch, q = 2 * y + zz // 4, zz % 4
+            ah = jnp.concatenate([uh[ch, q], uh[ch, q + 1]], axis=1)
+            al = jnp.concatenate([ul[ch, q], ul[ch, q + 1]], axis=1)
             out = dot(high, ah) + (dot(high, al) + dot(low, ah))
             for k in range(2):
                 start = y * RANK * 8 + zz + k
@@ -364,7 +382,7 @@
         pltpu.make_async_copy(cbuf.at[y], core_ref.at[:, y], out_sem.at[y]).wait()
 
 
-def project(u, gram):
+def project(uh, ul, gram):
     f32 = jnp.float32
     return pl.pallas_call(
         core_kernel,
@@ -373,23 +391,28 @@
             jax.ShapeDtypeStruct((RANK, NYD, 8, 128), f32),
             jax.ShapeDtypeStruct((ROWS, RANK), f32),
         ),
-        in_specs=[pl.BlockSpec(memory_space=pl.ANY), pl.BlockSpec(memory_space=pltpu.VMEM)],
+        in_specs=[
+            pl.BlockSpec(memory_space=pl.ANY),
+            pl.BlockSpec(memory_space=pl.ANY),
+            pl.BlockSpec(memory_space=pltpu.VMEM),
+        ],
         out_specs=(pl.BlockSpec(memory_space=pl.ANY), pl.BlockSpec(memory_space=pltpu.VMEM)),
         scratch_shapes=[
-            pltpu.VMEM((CHUNKS, 4, WIDE, 8, 128), f32),
+            pltpu.VMEM((CHUNKS, 4, ROWS, 128), jnp.bfloat16),
+            pltpu.VMEM((CHUNKS, 4, ROWS, 128), jnp.bfloat16),
             pltpu.VMEM((NYD, RANK, 8, 128), f32),
             pltpu.VMEM((RANK, ROWS), f32),
             pltpu.VMEM((512, 128), f32),
-            pltpu.SemaphoreType.DMA((CHUNKS,)),
+            pltpu.SemaphoreType.DMA((2, CHUNKS)),
             pltpu.SemaphoreType.DMA((NYD,)),
         ],
         compiler_params=pltpu.CompilerParams(vmem_limit_bytes=48 << 20),
-    )(u, gram)
+    )(uh, ul, gram)
 
 
 def on_device(snapshot):
-    u, gram = exchange_gram(snapshot)
-    return project(u, gram)
+    uh, ul, gram = exchange_gram(snapshot)
+    return project(uh, ul, gram)
 
 
 def solution(mesh):

time: 235 us -> 234 us (level)
  no operation moved by 1% of the time
where the time goes in v4:
time: 234 us
  Pallas kernels  234 us (100%)
    pallas_call x1, Pallas kernels, exchange_gram(): pl.pallas_call(exchange_gram_kernel, name='exchange_gram', out_shape=(jax...  218 us
    pallas_call x1, Pallas kernels, project(): pl.pallas_call(core_kernel, name='project', out_shape=(jax.ShapeDtypeStru...  16 us

profile of v4, /device:TPU:1, one launch (start us, length us, event | category | flops | bytes accessed | tf_op | source)
XLA Modules:
  0.0 234.2 jit_solution(17353870898590837904)
XLA Ops:
  0.6 217.6 %exchange_gram.1 = (bf16[8,4,512,128]{3,2,1,0:T(8,128)(2,1)S(1)}, bf16[8,4,512,128]{3,2,1,0:T(8,128)(2,1)}, f32[256,512]{1,0:T(8,128)S(1)}) custom-call(f32[8,4,512,128]{3,2,1,0:T(8,128)} %x_ref.1), custom_call_target="tpu_custom_call" | custom-call | tf_op jit(solution)/shard_map/exchange_gram/pallas_call | solution.py:219
  218.3 16.0 %project.1 = (f32[256,4,8,128]{3,2,1,0:T(8,128)}, f32[512,256]{1,0:T(8,128)}) custom-call(bf16[8,4,512,128]{3,2,1,0:T(8,128)(2,1)S(1)} %get-tuple-element.5.uh_ref, bf16[8,4,512,128]{3,2,1,0:T(8,128)(2,1)} %get-tuple-element.6.ul_ref, f32[256,512]{1,0:T(8,128)S(1)} %get-tuple-element.7.g_ref), custom_call_target="tpu_custom_call" | custom-call | tf_op jit(solution)/shard_map/project/pallas_call | solution.py:387

commit v5 on v3

--- a/solution.py
+++ b/solution.py
@@ -12,6 +12,10 @@
 NZD, NXD, NCD, NYD = 8, 4, 2, 4
 WIDE = NZD * NXD * NCD
 CHUNKS = 8
+PLANE = (
+    (2, 2), (2, 1), (2, 3), (1, 2), (3, 2), (1, 1), (1, 3), (3, 1),
+    (3, 3), (0, 2), (2, 0), (0, 1), (0, 3), (1, 0), (3, 0),
+)
 MESH = pl.DeviceIdType.MESH
 HIGHEST = lax.Precision.HIGHEST
 
@@ -19,7 +23,7 @@
 def exchange_gram_kernel(
     x_ref, u_ref, g_ref,
     xin, stag, ubuf, gacc, r1, h2, r2, r3, gfull,
-    in_sem, a_send, a_recv, out_sem, red_send, red_recv,
+    in_sem, a_send, a_recv, out_sem, red_send, red_recv, piece_recv,
 ):
     w = lax.axis_index("wide")
     y = lax.axis_index("narrow")
@@ -131,19 +135,12 @@
     pltpu.make_async_copy(r1, r1, red_recv.at[0]).wait()
     h2[...] = gacc[c] + r1[...]
 
-    def plane(i, stage, source, target):
-        t = (piece + i) % 16
+    for dx, dy in PLANE:
+        xx, yy = (x + dx) % NXD, (y + dy) % NYD
         pltpu.make_async_remote_copy(
-            src_ref=source(t), dst_ref=target, send_sem=red_send.at[stage],
-            recv_sem=red_recv.at[stage], device_id=(wide_id(z, t // NYD, c), t % NYD),
-            device_id_type=MESH,
+            src_ref=h2.at[xx * NYD + yy], dst_ref=r2.at[piece], send_sem=red_send.at[1],
+            recv_sem=red_recv.at[1], device_id=(wide_id(z, xx, c), yy), device_id_type=MESH,
         ).start()
-
-    def scatter(i, carry):
-        plane(i, 1, lambda t: h2.at[t], r2.at[piece])
-        return carry
-
-    lax.fori_loop(1, 16, scatter, 0)
     r2[piece] = h2[piece]
     got = r2.at[pl.ds(0, 15)]
     pltpu.make_async_copy(got, got, red_recv.at[1]).wait()
@@ -168,18 +165,24 @@
         total = total + r3[i]
     gfull[c, piece] = total
 
-    def gather(i, carry):
-        plane(i, 3, lambda t: gfull.at[c, piece], gfull.at[c, piece])
-        return carry
-
-    lax.fori_loop(1, 16, gather, 0)
-    got = gfull.at[c, pl.ds(0, 15)]
-    pltpu.make_async_copy(got, got, red_recv.at[3]).wait()
-    pltpu.make_async_remote_copy(
-        src_ref=gfull.at[c], dst_ref=gfull.at[c], send_sem=red_send.at[4],
-        recv_sem=red_recv.at[4], device_id=(partner, y), device_id_type=MESH,
-    ).start()
-    pltpu.make_async_copy(gfull.at[0], gfull.at[0], red_recv.at[4]).wait()
+    def across(p):
+        pltpu.make_async_remote_copy(
+            src_ref=gfull.at[c, p], dst_ref=gfull.at[c, p], send_sem=red_send.at[4],
+            recv_sem=red_recv.at[3], device_id=(partner, y), device_id_type=MESH,
+        ).start()
+
+    for dx, dy in PLANE:
+        xx, yy = (x + dx) % NXD, (y + dy) % NYD
+        pltpu.make_async_remote_copy(
+            src_ref=gfull.at[c, piece], dst_ref=gfull.at[c, piece], send_sem=red_send.at[3],
+            recv_sem=piece_recv.at[piece], device_id=(wide_id(z, xx, c), yy), device_id_type=MESH,
+        ).start()
+    across(piece)
+    for dx, dy in PLANE[::-1]:
+        p = ((x + NXD - dx) % NXD) * NYD + (y + NYD - dy) % NYD
+        pltpu.make_async_copy(gfull.at[c, p], gfull.at[c, p], piece_recv.at[p]).wait()
+        across(p)
+    pltpu.make_async_copy(gfull.at[0], gfull.at[0], red_recv.at[3]).wait()
     g_ref[...] = gfull[...].reshape(RANK, ROWS)
 
     def drain(ch, carry):
@@ -224,7 +227,7 @@
             pltpu.VMEM((16, 8, ROWS), f32),
             pltpu.VMEM((NZD, 8, ROWS), f32),
             pltpu.VMEM((2, 16, 8, ROWS), f32),
-            dma((4,)), dma((CHUNKS,)), dma((CHUNKS,)), dma((CHUNKS,)), dma((5,)), dma((5,)),
+            dma((4,)), dma((CHUNKS,)), dma((CHUNKS,)), dma((CHUNKS,)), dma((5,)), dma((4,)), dma((16,)),
         ],
         compiler_params=pltpu.CompilerParams(
             collective_id=0, has_side_effects=True, vmem_limit_bytes=48 << 20
@@ -334,7 +337,9 @@
     return high, (v - high.astype(jnp.float32)).astype(jnp.bfloat16)
 
 
-def core_kernel(u_ref, g_ref, core_ref, factor_ref, ubuf, cbuf, ft, tmp, in_sem, out_sem):
+def core_kernel(
+    u_ref, g_ref, core_ref, factor_ref, ubuf, cbuf, ft, fbuf, tmp, in_sem, out_sem
+):
     def begin(ch, carry):
         pltpu.make_async_copy(u_ref.at[ch], ubuf.at[ch], in_sem.at[ch]).start()
         return carry
@@ -359,9 +364,13 @@
                 start = y * RANK * 8 + zz + k
                 flat[pl.ds(start, RANK, stride=8), :] = out[:, 128 * k : 128 * k + 128]
         pltpu.make_async_copy(cbuf.at[y], core_ref.at[:, y], out_sem.at[y]).start()
-        factor_ref[128 * y : 128 * y + 128, :] = ft[:, 128 * y : 128 * y + 128].T
+        if y == 0:
+            for k in range(4):
+                fbuf[128 * k : 128 * k + 128, :] = ft[:, 128 * k : 128 * k + 128].T
+            pltpu.make_async_copy(fbuf, factor_ref, out_sem.at[NYD]).start()
     for y in range(NYD):
         pltpu.make_async_copy(cbuf.at[y], core_ref.at[:, y], out_sem.at[y]).wait()
+    pltpu.make_async_copy(fbuf, factor_ref, out_sem.at[NYD]).wait()
 
 
 def project(u, gram):
@@ -374,14 +383,15 @@
             jax.ShapeDtypeStruct((ROWS, RANK), f32),
         ),
         in_specs=[pl.BlockSpec(memory_space=pl.ANY), pl.BlockSpec(memory_space=pltpu.VMEM)],
-        out_specs=(pl.BlockSpec(memory_space=pl.ANY), pl.BlockSpec(memory_space=pltpu.VMEM)),
+        out_specs=(pl.BlockSpec(memory_space=pl.ANY), pl.BlockSpec(memory_space=pl.ANY)),
         scratch_shapes=[
             pltpu.VMEM((CHUNKS, 4, WIDE, 8, 128), f32),
             pltpu.VMEM((NYD, RANK, 8, 128), f32),
             pltpu.VMEM((RANK, ROWS), f32),
+            pltpu.VMEM((ROWS, RANK), f32),
             pltpu.VMEM((512, 128), f32),
             pltpu.SemaphoreType.DMA((CHUNKS,)),
-            pltpu.SemaphoreType.DMA((NYD,)),
+            pltpu.SemaphoreType.DMA((NYD + 1,)),
         ],
         compiler_params=pltpu.CompilerParams(vmem_limit_bytes=48 << 20),
     )(u, gram)

time: 235 us -> 233 us (level)
  no operation moved by 1% of the time
where the time goes in v5:
time: 233 us
  Pallas kernels  232 us (100%)
    pallas_call x1, Pallas kernels, exchange_gram(): pl.pallas_call(exchange_gram_kernel, name='exchange_gram', out_shape=(jax...  217 us
    pallas_call x1, Pallas kernels, project(): pl.pallas_call(core_kernel, name='project', out_shape=(jax.ShapeDtypeStru...  14.9 us

profile of v5, /device:TPU:1, one launch (start us, length us, event | category | flops | bytes accessed | tf_op | source)
XLA Modules:
  0.0 233.0 jit_solution(5244910188558757761)
XLA Ops:
  0.6 217.5 %exchange_gram.1 = (f32[8,4,64,8,128]{4,3,2,1,0:T(8,128)}, f32[256,512]{1,0:T(8,128)S(1)}) custom-call(f32[8,4,512,128]{3,2,1,0:T(8,128)} %x_ref.1), custom_call_target="tpu_custom_call" | custom-call | tf_op jit(solution)/shard_map/exchange_gram/pallas_call | solution.py:208
  218.1 14.9 %project.1 = (f32[256,4,8,128]{3,2,1,0:T(8,128)}, f32[512,256]{1,0:T(8,128)}) custom-call(f32[8,4,64,8,128]{4,3,2,1,0:T(8,128)} %get-tuple-element.4.u_ref, f32[256,512]{1,0:T(8,128)S(1)} %get-tuple-element.5.g_ref), custom_call_target="tpu_custom_call" | custom-call | tf_op jit(solution)/shard_map/project/pallas_call | solution.py:378

commit v6 on v5

--- a/solution.py
+++ b/solution.py
@@ -39,7 +39,8 @@
         pl.semaphore_signal(barrier, inc=1, device_id=((w + i) % WIDE, y), device_id_type=MESH)
         return carry
 
-    lax.fori_loop(1, WIDE, greet, 0)
+    lax.fori_loop(24, WIDE, greet, 0)
+    lax.fori_loop(1, 24, greet, 0)
 
     def greet_plane(i, carry):
         yy, xx = (y + 1 + i // NXD) % NYD, i % NXD

time: 233 us -> 233 us (level)
  no operation moved by 1% of the time
where the time goes in v6:
time: 233 us
  Pallas kernels  232 us (100%)
    pallas_call x1, Pallas kernels, exchange_gram(): pl.pallas_call(exchange_gram_kernel, name='exchange_gram', out_shape=(jax...  217 us
    pallas_call x1, Pallas kernels, project(): pl.pallas_call(core_kernel, name='project', out_shape=(jax.ShapeDtypeStru...  14.9 us

profile of v6, /device:TPU:1, one launch (start us, length us, event | category | flops | bytes accessed | tf_op | source)
XLA Modules:
  0.0 232.6 jit_solution(1854635376098115270)
XLA Ops:
  0.6 217.0 %exchange_gram.1 = (f32[8,4,64,8,128]{4,3,2,1,0:T(8,128)}, f32[256,512]{1,0:T(8,128)S(1)}) custom-call(f32[8,4,512,128]{3,2,1,0:T(8,128)} %x_ref.1), custom_call_target="tpu_custom_call" | custom-call | tf_op jit(solution)/shard_map/exchange_gram/pallas_call | solution.py:209
  217.6 14.9 %project.1 = (f32[256,4,8,128]{3,2,1,0:T(8,128)}, f32[512,256]{1,0:T(8,128)}) custom-call(f32[8,4,64,8,128]{4,3,2,1,0:T(8,128)} %get-tuple-element.4.u_ref, f32[256,512]{1,0:T(8,128)S(1)} %get-tuple-element.5.g_ref), custom_call_target="tpu_custom_call" | custom-call | tf_op jit(solution)/shard_map/project/pallas_call | solution.py:379
